TPU v7x, 512 devices: a whole 4x8x8 slice. The times are simulated.
512 devices in a mesh: dp: 128 (over z, y, core), rep: 4 (over x).
Axes of the slice: x: 4, y: 8, z: 8, core: 2. Of those that a mesh axis runs over, the one named last changes fastest.
Arguments:
- grads: bfloat16 [4, 128, 128, 4096], P('rep', 'dp')
- check_weights: int32 [4, 128, 8, 16], P('rep', 'dp'), may hold values from 1 to 8
Outputs:
- reduced: bfloat16 [128, 4096], P(None, 'dp')
- checksums: bfloat16 [8, 4096], P(None, 'dp')
All inputs are finite; a program needn't handle non-finite values.
Results may differ from a plain program's by a relative error of at most 0.0039.
Values may be sent and summed in bfloat16 or wider, within the bound.
A program may use at most 64 MiB of HBM per device.

v0:
```python
import jax
import jax.numpy as jnp
from jax import lax
from jax.sharding import Mesh
from jax.sharding import PartitionSpec as P

DP = ("dp_0", "dp_1", "dp_2")


def split_up(x, dim, peers):
    shape = x.shape
    tiles = x.reshape(*shape[:dim], peers, shape[dim] // peers, *shape[dim + 1 :])
    return jnp.moveaxis(tiles, dim, 0)


def sum_at_owner(x, axis, dim):
    peers = lax.axis_size(axis)
    tiles = lax.all_to_all(split_up(x, dim, peers), axis, 0, 0, tiled=True)
    return jnp.sum(tiles, axis=0)


def summed_rows(x, axes, dim):
    far, near = axes
    own = sum_at_owner(split_up(x, dim, lax.axis_size(far)), near, dim + 1)
    return jnp.sum(lax.all_to_all(own, far, 0, 0, tiled=True), axis=0)


def sent_together(arrays, axis, dim, along):
    ends, at = ([], 0)
    for a in arrays[:-1]:
        at += a.shape[along]
        ends.append(at)
    both = jnp.concatenate(arrays, axis=along)
    return tuple(jnp.split(summed_rows(both, axis, dim), ends, axis=along))


def sent_to_all(x, axis):
    peers = lax.axis_size(axis)
    return lax.all_to_all(jnp.broadcast_to(x[None], (peers, *x.shape)), axis, 0, 0, tiled=True)


def of_everyone(x, axis):
    return sent_to_all(x, axis).sum(axis=0)


def together(arrays, axis):
    vector, at, done = (jnp.concatenate([a.reshape(-1) for a in arrays]), 0, [])
    subtotal = of_everyone(vector, axis)
    for a in arrays:
        done.append(subtotal[at : at + a.size].reshape(a.shape))
        at += a.size
    return tuple(done)


def one_axis_at_a_time(x, axes):
    far, near = axes
    nearer = of_everyone(x, near)
    return of_everyone(nearer, far)


def encode(local_grad, weights):
    wsum = jnp.sum(weights, axis=-1).astype(jnp.float32)
    shaped = local_grad.reshape(weights.shape[0], weights.shape[1], local_grad.shape[-1])
    local = jnp.einsum(
        "kb,kbe->ke", weights.astype(jnp.bfloat16), shaped, preferred_element_type=jnp.float32
    )
    return local / wsum[:, None]


def clip_factor(square, total_rows, width):
    return jnp.minimum(
        1.0, 2.0 * jnp.sqrt(jnp.float32(total_rows * width)) / jnp.sqrt(square + 1e-06)
    )


def body(grads, check_weights):
    local_grad = grads[0, 0]
    local_check = encode(local_grad, check_weights[0, 0])
    terms = local_grad.astype(jnp.float32)
    total_rows = local_grad.shape[0]
    width = local_grad.shape[1]
    owned, owned_check = sent_together((terms, local_check), (("dp_0", "dp_1"), "dp_2"), 1, 0)
    owned, owned_check = together((owned, owned_check), "rep")
    square = one_axis_at_a_time(jnp.sum(owned * owned), (("dp_0", "dp_1"), "dp_2"))
    factor = clip_factor(square, total_rows, width)
    return ((factor * owned).astype(jnp.bfloat16), (factor * owned_check).astype(jnp.bfloat16))


def solution(mesh):
    torus = Mesh(mesh.devices.reshape(8, 8, 2, mesh.shape["rep"]), ("dp_0", "dp_1", "dp_2", "rep"))
    return jax.shard_map(
        body,
        mesh=torus,
        in_specs=(P("rep", DP, None, None), P("rep", DP, None, None)),
        out_specs=(P(None, DP), P(None, DP)),
        check_vma=False,
    )
```

profile of v0, /device:TPU:1, one launch (start us, length us, event | category | flops | bytes accessed | tf_op | source)
XLA Modules:
  0.0 136.9 jit_solution(15166288282575017443)
XLA Ops:
  0.6 0.0 copy-start
  0.6 0.9 fusion.3
  1.6 1.4 %bitcast_convert_fusion = f32[128,4096]{1,0:T(8,128)S(1)} fusion(bf16[1,1,128,4096]{3,2,1,0:T(8,128)(2,1)} %param.2), kind=kLoop, calls=%fused_computation.1 | loop fusion | flops 524288 | bytes 3145728 | tf_op jit(solution)/shard_map/convert_element_type | solution.py:79
  3.0 0.0 copy-done
  3.0 0.3 fusion
  3.3 0.1 bitcast_divide_fusion
  3.4 0.2 pad_maximum_fusion
  3.6 3.8 %reshape.58 = f32[136,64,64]{2,1,0:T(8,128)} reshape(f32[136,4096]{1,0:T(8,128)S(1)} %pad_maximum_fusion) | data formatting | bytes 4456448 | tf_op jit(solution)/shard_map/reshape | solution.py:12
  7.4 6.0 %copy.27 = f32[64,136,64]{1,2,0:T(8,128)} copy(f32[64,136,64]{2,0,1:T(8,128)} %bitcast.15) | data formatting | bytes 4456448 | tf_op jit(solution)/shard_map/transpose | solution.py:13
  13.3 2.5 %copy.28 = f32[2,64,136,32]{2,3,1,0:T(8,128)S(1)} copy(f32[2,64,136,32]{2,3,0,1:T(8,128)} %bitcast.16) | data formatting | bytes 4456448 | tf_op jit(solution)/shard_map/transpose | solution.py:13
  15.9 14.6 %all_to_all.28 = f32[2,64,136,32]{2,3,1,0:T(8,128)} all-to-all(f32[2,64,136,32]{2,3,1,0:T(8,128)S(1)} %copy.28), channel_id=1, replica_groups=mesh['dp_0'=8,'dp_1'=8,'dp_2'=2,'rep'=4] {'dp_2'}, dimensions={0} | all-to-all | bytes 4456448 | tf_op jit(solution)/shard_map/all_to_all | solution.py:18
  30.5 2.9 %reduce_sum.64 = f32[64,136,32]{1,2,0:T(8,128)S(1)} reduce(f32[2,64,136,32]{2,3,1,0:T(8,128)} %all_to_all.28, f32[]{:T(128)} %constant.2.clone.1), dimensions={0}, to_apply=%region_1.0 | reduce | flops 278528 | bytes 3342340 | tf_op jit(solution)/shard_map/reduce_sum | solution.py:19
  33.4 60.9 %all_to_all.29 = f32[64,136,32]{1,2,0:T(8,128)} all-to-all(f32[64,136,32]{1,2,0:T(8,128)S(1)} %reduce_sum.64), channel_id=1, replica_groups=mesh['dp_0'=8,'dp_1'=8,'dp_2'=2,'rep'=4] {'dp_0','dp_1'}, dimensions={0} | all-to-all | bytes 2228224 | tf_op jit(solution)/shard_map/all_to_all | solution.py:25
  94.3 1.8 %reduce_sum.65 = f32[136,32]{0,1:T(8,128)S(1)} reduce(f32[64,136,32]{1,2,0:T(8,128)} %all_to_all.29, f32[]{:T(128)} %constant.2.clone.1), dimensions={0}, to_apply=%region_2.0 | reduce | flops 274176 | bytes 1131524 | tf_op jit(solution)/shard_map/reduce_sum | solution.py:25
  96.1 0.1 copy.31
  96.2 0.1 reshape.61
  96.2 0.1 copy.30
  96.3 0.1 reshape.60
  96.5 8.3 %all_to_all.30 = f32[4,1,4352]{2,1,0:T(1,128)S(1)} all-to-all(f32[4,1,4352]{2,1,0:T(1,128)S(1)} %broadcast_in_dim.6), channel_id=1, replica_groups=mesh['dp_0'=8,'dp_1'=8,'dp_2'=2,'rep'=4] {'rep'}, dimensions={0} | all-to-all | bytes 139264 | tf_op jit(solution)/shard_map/all_to_all | solution.py:39
  104.8 0.1 reduce_sum.66
  104.9 0.6 multiply_reduce_fusion
  105.5 0.6 broadcast_in_dim.7
  106.1 8.4 %all_to_all.31 = f32[2,1,1]{2,1,0:T(1,128)S(1)} all-to-all(f32[2,1,1]{2,1,0:T(1,128)S(1)} %broadcast_in_dim.7), channel_id=1, replica_groups=mesh['dp_0'=8,'dp_1'=8,'dp_2'=2,'rep'=4] {'dp_2'}, dimensions={0} | all-to-all | bytes 16 | tf_op jit(solution)/shard_map/all_to_all | solution.py:39
  114.5 0.6 reduce_sum.68
  115.1 0.7 broadcast_in_dim.8
  115.8 18.3 %all_to_all.32 = f32[64,1,1]{2,1,0:T(1,128)S(1)} all-to-all(f32[64,1,1]{2,1,0:T(1,128)S(1)} %broadcast_in_dim.8), channel_id=1, replica_groups=mesh['dp_0'=8,'dp_1'=8,'dp_2'=2,'rep'=4] {'dp_0','dp_1'}, dimensions={0} | all-to-all | bytes 512 | tf_op jit(solution)/shard_map/all_to_all | solution.py:39
  134.1 0.7 reduce_sum.69
  135.4 0.7 convert_element_type.39
  136.1 0.1 convert_element_type.37
  136.2 0.7 copy.35
  (7 shorter events, 0.1 us)
Async XLA Ops:
  0.6 2.4 %copy-start = (bf16[1,1,128,4096]{3,2,1,0:T(8,128)(2,1)S(1)}, bf16[1,1,128,4096]{3,2,1,0:T(8,128)(2,1)}, u32[]{:S(2)}) copy-start(bf16[1,1,128,4096]{3,2,1,0:T(8,128)(2,1)} %param.2) | copy-start | bytes 3145732
where the time goes:
time: 137 us
  blocking collectives  111 us (81%)
  local copies, waits for them, and re-layouts  15.4 us (11%)
  other arithmetic  9.22 us (7%)
  between operations  1.46 us (1%)
    all_to_all x1, blocking collectives, summed_rows(): return jnp.sum(lax.all_to_all(own, far, 0, 0, tiled=True), axis=0)  60.9 us
    all_to_all x3, blocking collectives, sent_to_all(): lax.all_to_all(jnp.broadcast_to(x[None], (peers, *x.shape)), axis, 0, 0,...  35 us
    all_to_all x1, blocking collectives, sum_at_owner(): tiles = lax.all_to_all(split_up(x, dim, peers), axis, 0, 0, tiled=True)  14.6 us
    transpose x2, local copies, waits for them, and re-layouts, split_up(): return jnp.moveaxis(tiles, dim, 0)  8.48 us
    reshape x1, local copies, waits for them, and re-layouts, split_up(): x.reshape(*shape[:dim], peers, shape[dim] // peers, *shape[dim + 1:])  3.79 us
    reduce_sum x1, other arithmetic, sum_at_owner(): return jnp.sum(tiles, axis=0)  2.89 us

commit v1 on v0

v1 whole, which is shorter than its diff:
```python
import functools

import jax
import jax.numpy as jnp
from jax import lax
from jax.experimental import pallas as pl
from jax.experimental.pallas import tpu as pltpu
from jax.sharding import Mesh
from jax.sharding import PartitionSpec as P

MESH = pl.DeviceIdType.MESH
BF, F32 = jnp.bfloat16, jnp.float32
LANES = 128


def far_first(n):
    return sorted(range(1, n), key=lambda o: -min(o, n - o))


def kernel(sizes, limit, g_ref, w_ref, out_ref, chk_ref, own, par, wpar, sa, sb, ra, rb, sa2, sb2, ra2, rb2,
           x3, grp, nsend, nrm, xt, chk, own_sem, w_sem, s0_send, s0_recv, s1_send, s1_recv, s2_send, s2_recv,
           x_sem, g_sem, n_sem):
    Z, Y, X = sizes
    YH = Y // 2
    z, y, c, x = (lax.axis_index(a) for a in ("z", "y", "c", "x"))
    yh, p = y // 2, lax.rem(y, 2)
    other = 1 - c

    def remote(src, dst, send, recv, **at):
        return pltpu.make_async_remote_copy(
            src_ref=src, dst_ref=dst, send_sem=send, recv_sem=recv, device_id=at, device_id_type=MESH
        )

    def drained(ref, sem):
        pltpu.make_async_copy(ref, ref, sem).wait()

    half = pl.ds(pl.multiple_of(c * 64, 64), 64)
    mine = pltpu.make_async_copy(g_ref.at[half], own, own_sem)
    mine.start()

    barrier = pltpu.get_barrier_semaphore()
    pl.semaphore_signal(barrier, inc=1, device_id={"c": other}, device_id_type=MESH)
    for o in far_first(Y):
        pl.semaphore_signal(barrier, inc=1, device_id={"y": lax.rem(y + o, Y)}, device_id_type=MESH)
    for o in far_first(Z):
        pl.semaphore_signal(barrier, inc=1, device_id={"z": lax.rem(z + o, Z)}, device_id_type=MESH)
    for o in far_first(X):
        pl.semaphore_signal(barrier, inc=1, device_id={"x": lax.rem(x + o, X)}, device_id_type=MESH)
    twin = 2 * yh + 1 - p
    pl.semaphore_signal(barrier, inc=1, device_id={"y": twin, "c": other}, device_id_type=MESH)
    pl.semaphore_wait(barrier, Y + Z + X - 3 + 2)

    remote(w_ref, wpar, w_sem.at[0], w_sem.at[1], c=other).start()
    for q in (0, 2, 3, 1):
        rows = pl.ds(pl.multiple_of(other * 64 + 16 * q, 16), 16)
        remote(g_ref.at[rows], par.at[q], s0_send, s0_recv.at[q], c=other).start()

    eye = lax.broadcasted_iota(jnp.int32, (16, 16), 0) == lax.broadcasted_iota(jnp.int32, (16, 16), 1)

    def columns(ref):
        w = ref[...].astype(F32)
        w = w / jnp.sum(w, axis=1, keepdims=True)
        row = lax.broadcasted_iota(jnp.int32, w.shape, 0)
        cols = []
        for q in range(4):
            one = jnp.sum(jnp.where(row == 4 * c + q, w, 0.0), axis=0, keepdims=True)
            col = jnp.sum(jnp.where(eye, jnp.broadcast_to(one, (16, 16)), 0.0), axis=1, keepdims=True)
            cols.append(jnp.broadcast_to(col, (16, LANES)))
        return cols

    mine.wait()
    drained(w_ref, w_sem.at[1])
    w_own, w_par = columns(w_ref), columns(wpar)

    for q in (0, 2, 3, 1):
        drained(par.at[q], s0_recv.at[q])
        pq = q % 2
        for t in range(Z * YH):
            zt, yt = t // YH, t % YH
            lanes = slice(t * LANES, (t + 1) * LANES)
            a = own[16 * q : 16 * q + 16, lanes].astype(F32)
            b = par[q, :, lanes].astype(F32)
            both = (a + b).astype(BF)
            check = jnp.sum(a * w_own[q] + b * w_par[q], axis=0, keepdims=True)
            high = check.astype(BF)
            low = (check - high.astype(F32)).astype(BF)
            to, at, i, n = (sa, 2 * yt + pq, zt, Z) if q < 2 else (sb, zt, 2 * yt + pq, Y)
            to[at, 16 * i : 16 * i + 16, :] = both
            to[at, 16 * n + i : 16 * n + i + 1, :] = high
            to[at, 16 * n + 8 + i : 16 * n + 9 + i, :] = low
        if q == 3:
            for o in far_first(Z):
                to = lax.rem(z + o, Z)
                remote(sb.at[to], rb.at[o - 1], s1_send.at[1], s1_recv.at[1], z=to).start()
        if q == 1:
            for o in far_first(Y):
                to = lax.rem(y + o, Y)
                remote(sa.at[to], ra.at[o - 1], s1_send.at[0], s1_recv.at[0], y=to).start()

    def fold(s, r, me, n, s2):
        def block(t):
            rows = slice(16 * t, 16 * t + 16)
            acc = s[me, rows, :].astype(F32)
            for o in range(r.shape[0]):
                acc += r[o, rows, :].astype(F32)
            return acc

        for t in range(n):
            s2[t, 0:16, :] = block(t)
        last = block(n)
        check = last[0:8] + last[8:16]
        for t in range(n):
            s2[t, 16:24, :] = jnp.broadcast_to(check[t : t + 1], (8, LANES))

    drained(rb, s1_recv.at[1])
    fold(sb, rb, z, Y, sb2)
    for o in far_first(Y):
        to = lax.rem(y + o, Y)
        remote(sb2.at[to], rb2.at[o - 1], s2_send.at[1], s2_recv.at[1], y=to).start()
    drained(ra, s1_recv.at[0])
    fold(sa, ra, y, Z, sa2)
    for o in far_first(Z):
        to = lax.rem(z + o, Z)
        remote(sa2.at[to], ra2.at[o - 1], s2_send.at[0], s2_recv.at[0], z=to).start()

    def total(s2, r2, me):
        acc = s2[me]
        for o in range(r2.shape[0]):
            acc += r2[o]
        return acc

    drained(rb2, s2_recv.at[1])
    low_rows = total(sb2, rb2, y)
    drained(ra2, s2_recv.at[0])
    top_rows = total(sa2, ra2, z)
    x3[x, 0:16, :] = top_rows[0:16]
    x3[x, 16:32, :] = low_rows[0:16]
    row = lax.broadcasted_iota(jnp.int32, (8, LANES), 0)
    x3[x, 32:40, :] = jnp.where(row < 4, top_rows[16:24], low_rows[16:24])
    for o in far_first(X):
        remote(x3.at[x], x3.at[x], x_sem.at[0], x_sem.at[1], x=lax.rem(x + o, X)).start()
    drained(x3.at[pl.ds(0, X - 1)], x_sem.at[1])
    m = 2 * p + c
    acc = x3[0]
    for i in range(1, X):
        acc += x3[i]
    grp[m] = acc
    for at in ({"y": twin}, {"c": other}, {"y": twin, "c": other}):
        remote(grp.at[m], grp.at[m], g_sem.at[0], g_sem.at[1], **at).start()
    drained(grp.at[pl.ds(0, 3)], g_sem.at[1])

    parts = []
    for i in range(8):
        core, q = i // 4, i % 4
        parts.append(grp[2 * (q % 2) + core, 16 * (q // 2) : 16 * (q // 2) + 16, :])
    whole = jnp.concatenate(parts, axis=0)
    nsend[...] = jnp.sum(whole * whole, axis=0, keepdims=True)
    j = 0
    order = sorted(
        ((a, b) for a in range(Z) for b in range(YH) if a or b),
        key=lambda o: -(min(o[0], Z - o[0]) + 2 * min(o[1], YH - o[1])),
    )
    for dz, dy in order:
        at = {"z": lax.rem(z + dz, Z), "y": lax.rem(y + 2 * dy, Y)}
        remote(nsend, nrm.at[j], n_sem.at[0], n_sem.at[1], **at).start()
        j += 1

    xt[...] = whole.T
    for k in range(8):
        core, q = k // 4, k % 4
        r = 32 + 4 * (q // 2)
        chk[k : k + 1, :] = grp[2 * (q % 2) + core, r : r + 1, :]
    turned = pltpu.roll(chk[...], lax.rem(LANES - 32 * m, LANES), 1)[:, 0:32]
    columns_out = xt[pl.ds(pl.multiple_of(32 * m, 32), 32), :]

    drained(nrm, n_sem.at[1])
    square = nsend[...]
    square += jnp.sum(nrm[...], axis=0)
    square = jnp.sum(square, axis=1, keepdims=True)
    factor = jnp.minimum(1.0, limit / jnp.sqrt(square + 1e-06))
    out_ref[...] = (columns_out * factor).astype(BF)
    chk_ref[...] = (turned * factor).astype(BF)

    drained(w_ref, w_sem.at[0])
    drained(par, s0_send)
    drained(ra, s1_send.at[0])
    drained(rb, s1_send.at[1])
    drained(ra2, s2_send.at[0])
    drained(rb2, s2_send.at[1])
    drained(x3.at[pl.ds(0, X - 1)], x_sem.at[0])
    drained(grp.at[pl.ds(0, 3)], g_sem.at[0])
    drained(nrm, n_sem.at[0])


def body(sizes, grads, check_weights):
    Z, Y, X = sizes
    local, weights = grads[0, 0], check_weights[0, 0]
    rows, width = local.shape
    limit = 2.0 * float((rows * Z * (Y // 2) * LANES) ** 0.5)
    dma = pltpu.SemaphoreType.DMA
    vmem = pltpu.VMEM
    out, chk = pl.pallas_call(
        functools.partial(kernel, sizes, limit),
        out_shape=(jax.ShapeDtypeStruct((32, rows), BF), jax.ShapeDtypeStruct((8, 32), BF)),
        in_specs=[pl.BlockSpec(memory_space=pl.ANY), pl.BlockSpec(memory_space=vmem)],
        out_specs=(pl.BlockSpec(memory_space=vmem), pl.BlockSpec(memory_space=vmem)),
        scratch_shapes=[
            vmem((64, width), BF),
            vmem((4, 16, width), BF),
            vmem((8, 16), jnp.int32),
            vmem((Y, 16 * Z + 16, LANES), BF),
            vmem((Z, 16 * Y + 16, LANES), BF),
            vmem((Y - 1, 16 * Z + 16, LANES), BF),
            vmem((Z - 1, 16 * Y + 16, LANES), BF),
            vmem((Z, 24, LANES), F32),
            vmem((Y, 24, LANES), F32),
            vmem((Z - 1, 24, LANES), F32),
            vmem((Y - 1, 24, LANES), F32),
            vmem((X, 40, LANES), F32),
            vmem((4, 40, LANES), F32),
            vmem((1, LANES), F32),
            vmem((Z * (Y // 2) - 1, 1, LANES), F32),
            vmem((LANES, LANES), F32),
            vmem((8, LANES), F32),
            dma,
            dma((2,)),
            dma,
            dma((4,)),
            dma((2,)),
            dma((2,)),
            dma((2,)),
            dma((2,)),
            dma((2,)),
            dma((2,)),
            dma((2,)),
        ],
        compiler_params=pltpu.CompilerParams(collective_id=0, has_side_effects=True),
    )(local, weights)
    return out.T, chk


def solution(mesh):
    Z, Y, X = 8, 8, mesh.shape["rep"]
    torus = Mesh(mesh.devices.reshape(Z, Y, 2, X), ("z", "y", "c", "x"))
    dp = ("z", "y", "c")
    return jax.shard_map(
        functools.partial(body, (Z, Y, X)),
        mesh=torus,
        in_specs=(P("x", dp, None, None), P("x", dp, None, None)),
        out_specs=(P(None, dp), P(None, dp)),
        check_vma=False,
    )
```

time: 137 us -> 47.8 us (0.35)
  blocking collectives: 111 us -> 0 us
  Pallas kernels: 0 us -> 45 us
  local copies, waits for them, and re-layouts: 15.4 us -> 1.88 us
  other arithmetic: 9.22 us -> 0 us
    all_to_all x5 -> x0, blocking collectives: 111 us -> none  [the longest x1 60.9 us: summed_rows(): return jnp.sum(lax.all_to_all(own, far, 0, 0, tiled=True), axis=0)]
    pallas_call x0 -> x1, Pallas kernels: none -> 45 us  [body(): pl.pallas_call(functools.partial(kernel, sizes, limit), out_shape=(jax.Sh...]
    transpose x2 -> x0, local copies, waits for them, and re-layouts: 8.48 us -> none  [split_up(): return jnp.moveaxis(tiles, dim, 0)]
    reduce_sum x7 -> x0, other arithmetic: 7.5 us -> none  [the longest x1 2.89 us: sum_at_owner(): return jnp.sum(tiles, axis=0)]
    reshape x3 -> x0, local copies, waits for them, and re-layouts: 3.95 us -> none  [the longest x1 3.79 us: split_up(): x.reshape(*shape[:dim], peers, shape[dim] // peers, *shape[dim + 1:])]
    convert_element_type x4 -> x0, other arithmetic: 1.44 us -> none  [the longest x1 1.42 us: body(): terms = local_grad.astype(jnp.float32)]
where the time goes in v1:
time: 47.8 us; the launch traced here: 47.6 us
  Pallas kernels  45 us (94%)
  local copies, waits for them, and re-layouts  1.88 us (4%)
  between operations  0.65 us (1%)
    pallas_call x1, Pallas kernels, body(): pl.pallas_call(functools.partial(kernel, sizes, limit), out_shape=(jax.Sh...  45 us
    unnamed x4, local copies, waits for them, and re-layouts  1.88 us

profile of v1, /device:TPU:1, one launch (start us, length us, event | category | flops | bytes accessed | tf_op | source)
XLA Modules:
  0.0 47.6 jit_solution(9427035392682184660)
XLA Ops:
  0.6 45.0 %shard_map.41 = (bf16[32,128]{1,0:T(8,128)(2,1)}, bf16[8,32]{1,0:T(8,128)(2,1)}) custom-call(bf16[128,4096]{1,0:T(8,128)(2,1)} %bitcast.3, s32[8,16]{1,0:T(8,128)} %bitcast.5), custom_call_target="tpu_custom_call" | custom-call | tf_op jit(solution)/shard_map/pallas_call | solution.py:202
  45.7 0.0 copy-start
  45.7 1.3 %copy.6 = bf16[128,32]{0,1:T(8,128)(2,1)} copy(bf16[128,32]{0,1:T(8,128)(2,1)} %bitcast.4) | data formatting | bytes 16384
  47.0 0.0 copy-done
  47.0 0.6 %copy.7 = bf16[8,32]{1,0:T(8,128)(2,1)} copy(bf16[8,32]{1,0:T(8,128)(2,1)S(1)} %copy-done) | data formatting | bytes 1024
Async XLA Ops:
  45.7 1.3 %copy-start = (bf16[8,32]{1,0:T(8,128)(2,1)S(1)}, bf16[8,32]{1,0:T(8,128)(2,1)}, u32[]{:S(2)}) copy-start(bf16[8,32]{1,0:T(8,128)(2,1)} %get-tuple-element.9) | copy-start | bytes 1540

commit v2 on v1

v2 whole, which is shorter than its diff:
```python
import functools

import jax
import jax.numpy as jnp
from jax import lax
from jax.experimental import pallas as pl
from jax.experimental.pallas import tpu as pltpu
from jax.sharding import Mesh
from jax.sharding import PartitionSpec as P

MESH = pl.DeviceIdType.MESH
BF, F32 = jnp.bfloat16, jnp.float32
LANES = 128
HBM = pltpu.MemorySpace.HBM


def far_first(n):
    return sorted(range(1, n), key=lambda o: -min(o, n - o))


def near(n):
    return [o for o in far_first(n) if min(o, n - o) <= 2]


def kernel(sizes, limit, g_ref, w_ref, out_ref, chk_ref, own, par, wown, wpar, sa, sb, ra, rb, ca, cb, rca, rcb,
           sa2, sb2, ra2, rb2, ca2, cb2, rca2, rcb2, x3, xc, grp, gc, nsend, nrm, xt, chk, own_sem, w_sem, hop,
           s0_send, s0_recv, s1_send, s1_recv, c1_send, c1_recv, s2_send, s2_recv, c2_send, c2_recv,
           x_sem, g_sem, n_sem):
    Z, Y, X = sizes
    YH = Y // 2
    z, y, c, x = (lax.axis_index(a) for a in ("z", "y", "c", "x"))
    yh, p = y // 2, lax.rem(y, 2)
    other = 1 - c

    def remote(src, dst, send, recv, at):
        pltpu.make_async_remote_copy(
            src_ref=src, dst_ref=dst, send_sem=send, recv_sem=recv, device_id=at, device_id_type=MESH
        ).start()

    def signal(sem, at):
        pl.semaphore_signal(sem, inc=1, device_id=at, device_id_type=MESH)

    def drained(ref, sem):
        pltpu.make_async_copy(ref, ref, sem).wait()

    half = pl.ds(pl.multiple_of(c * 64, 64), 64)
    weights = pltpu.make_async_copy(w_ref, wown, w_sem.at[2])
    weights.start()
    mine = pltpu.make_async_copy(g_ref.at[half], own, own_sem)
    mine.start()

    barrier = pltpu.get_barrier_semaphore()
    for o in near(Y):
        signal(barrier, {"y": lax.rem(y + o, Y)})
    for o in near(Z):
        signal(barrier, {"z": lax.rem(z + o, Z)})
    for o in far_first(X):
        signal(barrier, {"x": lax.rem(x + o, X)})
    signal(barrier, {"c": other})
    pl.semaphore_wait(barrier, len(near(Y)) + len(near(Z)) + X)

    for o in near(Y):
        signal(hop.at[0], {"y": lax.rem(y + o, Y)})
    for o in near(Z):
        signal(hop.at[1], {"z": lax.rem(z + o, Z)})
    for q in (0, 2, 3, 1):
        rows = pl.ds(pl.multiple_of(other * 64 + 16 * q, 16), 16)
        remote(g_ref.at[rows], par.at[q], s0_send, s0_recv.at[q], {"c": other})
    weights.wait()
    remote(wown, wpar, w_sem.at[0], w_sem.at[1], {"c": other})

    eye = lax.broadcasted_iota(jnp.int32, (16, 16), 0) == lax.broadcasted_iota(jnp.int32, (16, 16), 1)

    def columns(ref):
        w = ref[...].astype(F32)
        w = w / jnp.sum(w, axis=1, keepdims=True)
        row = lax.broadcasted_iota(jnp.int32, w.shape, 0)
        cols = []
        for q in range(4):
            one = jnp.sum(jnp.where(row == 4 * c + q, w, 0.0), axis=0, keepdims=True)
            col = jnp.sum(jnp.where(eye, jnp.broadcast_to(one, (16, 16)), 0.0), axis=1, keepdims=True)
            cols.append(jnp.broadcast_to(col, (16, LANES)))
        return cols

    w_own = columns(wown)
    mine.wait()
    drained(wpar, w_sem.at[1])
    w_par = columns(wpar)

    for q in (0, 2, 3, 1):
        drained(par.at[q], s0_recv.at[q])
        for t in range(Z * YH):
            zt, yt = t // YH, t % YH
            lanes = slice(t * LANES, (t + 1) * LANES)
            a = own[16 * q : 16 * q + 16, lanes].astype(F32)
            b = par[q, :, lanes].astype(F32)
            check = jnp.sum(a * w_own[q] + b * w_par[q], axis=0, keepdims=True)
            to, cto, at, i = (sa, ca, 2 * yt + q, zt) if q < 2 else (sb, cb, zt, 2 * yt + q - 2)
            to[at, 16 * i : 16 * i + 16, :] = (a + b).astype(BF)
            cto[at, i : i + 1, :] = check.astype(BF)
        if q == 3:
            pl.semaphore_wait(hop.at[1], len(near(Z)))
            for o in far_first(Z):
                to = lax.rem(z + o, Z)
                remote(sb.at[to], rb.at[o - 1], s1_send.at[1], s1_recv.at[1], {"z": to})
                remote(cb.at[to], rcb.at[o - 1], c1_send.at[1], c1_recv.at[1], {"z": to})
        if q == 1:
            pl.semaphore_wait(hop.at[0], len(near(Y)))
            for o in far_first(Y):
                to = lax.rem(y + o, Y)
                remote(sa.at[to], ra.at[o - 1], s1_send.at[0], s1_recv.at[0], {"y": to})
                remote(ca.at[to], rca.at[o - 1], c1_send.at[0], c1_recv.at[0], {"y": to})

    def fold(s, r, cs, cr, me, n, s2, c2):
        for t in range(n):
            rows = slice(16 * t, 16 * t + 16)
            acc = s[me, rows, :].astype(F32)
            for o in range(r.shape[0]):
                acc += r[o, rows, :].astype(F32)
            s2[t] = acc
        check = cs[me].astype(F32)
        for o in range(r.shape[0]):
            check += cr[o].astype(F32)
        for t in range(n):
            c2[t] = check[t : t + 1]

    drained(rb, s1_recv.at[1])
    drained(rcb, c1_recv.at[1])
    fold(sb, rb, cb, rcb, z, Y, sb2, cb2)
    for o in far_first(Y):
        to = lax.rem(y + o, Y)
        remote(sb2.at[to], rb2.at[o - 1], s2_send.at[1], s2_recv.at[1], {"y": to})
        remote(cb2.at[to], rcb2.at[o - 1], c2_send.at[1], c2_recv.at[1], {"y": to})
    drained(ra, s1_recv.at[0])
    drained(rca, c1_recv.at[0])
    fold(sa, ra, ca, rca, y, Z, sa2, ca2)
    for o in far_first(Z):
        to = lax.rem(z + o, Z)
        remote(sa2.at[to], ra2.at[o - 1], s2_send.at[0], s2_recv.at[0], {"z": to})
        remote(ca2.at[to], rca2.at[o - 1], c2_send.at[0], c2_recv.at[0], {"z": to})

    def total(s2, r2, me):
        acc = s2[me]
        for o in range(r2.shape[0]):
            acc += r2[o]
        return acc

    drained(rb2, s2_recv.at[1])
    drained(rcb2, c2_recv.at[1])
    x3[x, 16:32, :] = total(sb2, rb2, y)
    xc[x, 1] = total(cb2, rcb2, y)
    drained(ra2, s2_recv.at[0])
    drained(rca2, c2_recv.at[0])
    x3[x, 0:16, :] = total(sa2, ra2, z)
    xc[x, 0] = total(ca2, rca2, z)
    for o in far_first(X):
        at = {"x": lax.rem(x + o, X)}
        remote(x3.at[x], x3.at[x], x_sem.at[0], x_sem.at[1], at)
        remote(xc.at[x], xc.at[x], x_sem.at[2], x_sem.at[3], at)
    drained(x3.at[pl.ds(0, X - 1)], x_sem.at[1])
    drained(xc.at[pl.ds(0, X - 1)], x_sem.at[3])
    m = 2 * p + c
    acc, check = x3[0], xc[0]
    for i in range(1, X):
        acc += x3[i]
        check += xc[i]

    nsend[...] = jnp.sum(acc * acc, axis=0, keepdims=True)
    grp[m] = acc
    gc[m] = check
    order = sorted(
        ((a, b, k) for a in range(Z) for b in range(Y) for k in range(2) if a or b or k),
        key=lambda o: -(min(o[0], Z - o[0]) + min(o[1], Y - o[1])),
    )
    for j, (dz, dy, dc) in enumerate(order):
        at = {"z": lax.rem(z + dz, Z), "y": lax.rem(y + dy, Y), "c": lax.rem(c + dc, 2)}
        remote(nsend, nrm.at[j], n_sem.at[0], n_sem.at[1], at)
    twin = 2 * yh + 1 - p
    for at in ({"y": twin, "c": other}, {"y": twin, "c": c}, {"y": y, "c": other}):
        remote(grp.at[m], grp.at[m], g_sem.at[0], g_sem.at[1], at)
        remote(gc.at[m], gc.at[m], g_sem.at[2], g_sem.at[3], at)
    drained(grp.at[pl.ds(0, 3)], g_sem.at[1])
    drained(gc.at[pl.ds(0, 3)], g_sem.at[3])
    parts = []
    for i in range(8):
        core, q = i // 4, i % 4
        parts.append(grp[2 * (q % 2) + core, 16 * (q // 2) : 16 * (q // 2) + 16, :])
        chk[i : i + 1, :] = gc[2 * (q % 2) + core, q // 2]
    xt[...] = jnp.concatenate(parts, axis=0).T
    turned = pltpu.roll(chk[...], lax.rem(LANES - 32 * m, LANES), 1)[:, 0:32]
    columns_out = xt[pl.ds(pl.multiple_of(32 * m, 32), 32), :]

    drained(nrm, n_sem.at[1])
    square = nsend[...] + jnp.sum(nrm[...], axis=0)
    square = jnp.sum(square, axis=1, keepdims=True)
    factor = jnp.minimum(1.0, limit / jnp.sqrt(square + 1e-06))
    out_ref[...] = (columns_out * factor).astype(BF)
    chk_ref[...] = (turned * factor).astype(BF)

    drained(wown, w_sem.at[0])
    drained(par, s0_send)
    for ref, sem in (
        (ra, s1_send.at[0]), (rb, s1_send.at[1]), (rca, c1_send.at[0]), (rcb, c1_send.at[1]),
        (ra2, s2_send.at[0]), (rb2, s2_send.at[1]), (rca2, c2_send.at[0]), (rcb2, c2_send.at[1]),
        (x3.at[pl.ds(0, X - 1)], x_sem.at[0]), (xc.at[pl.ds(0, X - 1)], x_sem.at[2]),
        (grp.at[pl.ds(0, 3)], g_sem.at[0]), (gc.at[pl.ds(0, 3)], g_sem.at[2]), (nrm, n_sem.at[0]),
    ):
        drained(ref, sem)


def body(sizes, grads, check_weights):
    Z, Y, X = sizes
    local, weights = grads[0, 0], check_weights[0, 0]
    rows, width = local.shape
    limit = 2.0 * float((rows * Z * (Y // 2) * LANES) ** 0.5)
    dma = pltpu.SemaphoreType.DMA
    vmem = pltpu.VMEM
    out, chk = pl.pallas_call(
        functools.partial(kernel, sizes, limit),
        out_shape=(jax.ShapeDtypeStruct((32, rows), BF), jax.ShapeDtypeStruct((8, 32), BF)),
        in_specs=[pl.BlockSpec(memory_space=HBM)] * 2,
        out_specs=(pl.BlockSpec(memory_space=vmem), pl.BlockSpec(memory_space=vmem)),
        scratch_shapes=[
            vmem((64, width), BF),
            vmem((4, 16, width), BF),
            vmem((8, 16), jnp.int32),
            vmem((8, 16), jnp.int32),
            *(vmem((n, 16 * k, LANES), BF) for n, k in ((Y, Z), (Z, Y), (Y - 1, Z), (Z - 1, Y))),
            *(vmem((n, 8, LANES), BF) for n in (Y, Z, Y - 1, Z - 1)),
            *(vmem((n, 16, LANES), F32) for n in (Z, Y, Z - 1, Y - 1)),
            *(vmem((n, 1, LANES), F32) for n in (Z, Y, Z - 1, Y - 1)),
            vmem((X, 32, LANES), F32),
            vmem((X, 2, 1, LANES), F32),
            vmem((4, 32, LANES), F32),
            vmem((4, 2, 1, LANES), F32),
            vmem((1, LANES), F32),
            vmem((Z * Y * 2 - 1, 1, LANES), F32),
            vmem((LANES, LANES), F32),
            vmem((8, LANES), F32),
            dma,
            dma((3,)),
            pltpu.SemaphoreType.REGULAR((2,)),
            dma,
            dma((4,)),
            *(dma((2,)) for _ in range(8)),
            dma((4,)),
            dma((4,)),
            dma((2,)),
        ],
        compiler_params=pltpu.CompilerParams(collective_id=0, has_side_effects=True, vmem_limit_bytes=8 << 20),
    )(pltpu.with_memory_space_constraint(local, HBM), pltpu.with_memory_space_constraint(weights, HBM))
    return out.T, chk


def solution(mesh):
    Z, Y, X = 8, 8, mesh.shape["rep"]
    torus = Mesh(mesh.devices.reshape(Z, Y, 2, X), ("z", "y", "c", "x"))
    dp = ("z", "y", "c")
    return jax.shard_map(
        functools.partial(body, (Z, Y, X)),
        mesh=torus,
        in_specs=(P("x", dp, None, None), P("x", dp, None, None)),
        out_specs=(P(None, dp), P(None, dp)),
        check_vma=False,
    )
```

time: 47.8 us -> 43.4 us (0.908)
  Pallas kernels: 45 us -> 41.5 us
  local copies, waits for them, and re-layouts: 1.88 us -> 1.18 us
    pallas_call x1, Pallas kernels: 45 us -> 41.5 us  [body(): pl.pallas_call(functools.partial(kernel, sizes, limit), out_shape=(jax.Sh...]
    unnamed x4 -> x2, local copies, waits for them, and re-layouts: 1.88 us -> 1.18 us
where the time goes in v2:
time: 43.4 us; the launch traced here: 43.3 us
  Pallas kernels  41.5 us (96%)
  local copies, waits for them, and re-layouts  1.18 us (3%)
  between operations  0.64 us (1%)
    pallas_call x1, Pallas kernels, body(): pl.pallas_call(functools.partial(kernel, sizes, limit), out_shape=(jax.Sh...  41.5 us
    unnamed x2, local copies, waits for them, and re-layouts  1.18 us

profile of v2, /device:TPU:1, one launch (start us, length us, event | category | flops | bytes accessed | tf_op | source)
XLA Modules:
  0.0 43.3 jit_solution(5959829098649841943)
XLA Ops:
  0.6 41.5 %shard_map.41 = (bf16[32,128]{1,0:T(8,128)(2,1)S(1)}, bf16[8,32]{1,0:T(8,128)(2,1)S(1)}) custom-call(bf16[128,4096]{1,0:T(8,128)(2,1)} %bitcast.4, s32[8,16]{1,0:T(8,128)} %bitcast.5), custom_call_target="tpu_custom_call" | custom-call | tf_op jit(solution)/shard_map/pallas_call | solution.py:218
  42.1 0.6 %copy.6 = bf16[128,32]{0,1:T(8,128)(2,1)} copy(bf16[128,32]{0,1:T(8,128)(2,1)S(1)} %bitcast.3) | data formatting | bytes 16384
  42.7 0.6 %copy.7 = bf16[8,32]{1,0:T(8,128)(2,1)} copy(bf16[8,32]{1,0:T(8,128)(2,1)S(1)} %get-tuple-element.9) | data formatting | bytes 1024

commit v3 on v2

--- a/solution.py
+++ b/solution.py
@@ -23,9 +23,9 @@
 
 
 def kernel(sizes, limit, g_ref, w_ref, out_ref, chk_ref, own, par, wown, wpar, sa, sb, ra, rb, ca, cb, rca, rcb,
-           sa2, sb2, ra2, rb2, ca2, cb2, rca2, rcb2, x3, xc, grp, gc, nsend, nrm, xt, chk, own_sem, w_sem, hop,
+           sa2, sb2, ra2, rb2, ca2, cb2, rca2, rcb2, grp, gc, nsend, nrm, xt, chk, own_sem, w_sem, hop,
            s0_send, s0_recv, s1_send, s1_recv, c1_send, c1_recv, s2_send, s2_recv, c2_send, c2_recv,
-           x_sem, g_sem, n_sem):
+           g_sem, n_sem):
     Z, Y, X = sizes
     YH = Y // 2
     z, y, c, x = (lax.axis_index(a) for a in ("z", "y", "c", "x"))
@@ -66,8 +66,7 @@
     for q in (0, 2, 3, 1):
         rows = pl.ds(pl.multiple_of(other * 64 + 16 * q, 16), 16)
         remote(g_ref.at[rows], par.at[q], s0_send, s0_recv.at[q], {"c": other})
-    weights.wait()
-    remote(wown, wpar, w_sem.at[0], w_sem.at[1], {"c": other})
+    remote(w_ref, wpar, w_sem.at[0], w_sem.at[1], {"c": other})
 
     eye = lax.broadcasted_iota(jnp.int32, (16, 16), 0) == lax.broadcasted_iota(jnp.int32, (16, 16), 1)
 
@@ -82,6 +81,7 @@
             cols.append(jnp.broadcast_to(col, (16, LANES)))
         return cols
 
+    weights.wait()
     w_own = columns(wown)
     mine.wait()
     drained(wpar, w_sem.at[1])
@@ -111,63 +111,68 @@
                 remote(sa.at[to], ra.at[o - 1], s1_send.at[0], s1_recv.at[0], {"y": to})
                 remote(ca.at[to], rca.at[o - 1], c1_send.at[0], c1_recv.at[0], {"y": to})
 
-    def fold(s, r, cs, cr, me, n, s2, c2):
-        for t in range(n):
-            rows = slice(16 * t, 16 * t + 16)
-            acc = s[me, rows, :].astype(F32)
-            for o in range(r.shape[0]):
-                acc += r[o, rows, :].astype(F32)
-            s2[t] = acc
-        check = cs[me].astype(F32)
-        for o in range(r.shape[0]):
+    def fold(k, axis, held, me, n, s, r, cs, cr, s2, r2, c2, cr2):
+        drained(cr, c1_recv.at[k])
+        check = cs[held].astype(F32)
+        for o in range(cr.shape[0]):
             check += cr[o].astype(F32)
         for t in range(n):
             c2[t] = check[t : t + 1]
-
-    drained(rb, s1_recv.at[1])
-    drained(rcb, c1_recv.at[1])
-    fold(sb, rb, cb, rcb, z, Y, sb2, cb2)
-    for o in far_first(Y):
-        to = lax.rem(y + o, Y)
-        remote(sb2.at[to], rb2.at[o - 1], s2_send.at[1], s2_recv.at[1], {"y": to})
-        remote(cb2.at[to], rcb2.at[o - 1], c2_send.at[1], c2_recv.at[1], {"y": to})
-    drained(ra, s1_recv.at[0])
-    drained(rca, c1_recv.at[0])
-    fold(sa, ra, ca, rca, y, Z, sa2, ca2)
-    for o in far_first(Z):
-        to = lax.rem(z + o, Z)
-        remote(sa2.at[to], ra2.at[o - 1], s2_send.at[0], s2_recv.at[0], {"z": to})
-        remote(ca2.at[to], rca2.at[o - 1], c2_send.at[0], c2_recv.at[0], {"z": to})
-
-    def total(s2, r2, me):
-        acc = s2[me]
-        for o in range(r2.shape[0]):
-            acc += r2[o]
-        return acc
-
-    drained(rb2, s2_recv.at[1])
-    drained(rcb2, c2_recv.at[1])
-    x3[x, 16:32, :] = total(sb2, rb2, y)
-    xc[x, 1] = total(cb2, rcb2, y)
-    drained(ra2, s2_recv.at[0])
-    drained(rca2, c2_recv.at[0])
-    x3[x, 0:16, :] = total(sa2, ra2, z)
-    xc[x, 0] = total(ca2, rca2, z)
-    for o in far_first(X):
-        at = {"x": lax.rem(x + o, X)}
-        remote(x3.at[x], x3.at[x], x_sem.at[0], x_sem.at[1], at)
-        remote(xc.at[x], xc.at[x], x_sem.at[2], x_sem.at[3], at)
-    drained(x3.at[pl.ds(0, X - 1)], x_sem.at[1])
-    drained(xc.at[pl.ds(0, X - 1)], x_sem.at[3])
+        if k:
+            drained(r, s1_recv.at[k])
+        slot = x * n + me
+
+        def block(o):
+            to = lax.rem(me + o, n)
+            rows = pl.ds(pl.multiple_of(16 * to, 16), 16)
+            acc = s[held, rows, :].astype(F32)
+            for i in range(r.shape[0]):
+                acc += r[i, rows, :].astype(F32)
+            s2[to] = acc.astype(BF)
+
+        def send(o):
+            to = lax.rem(me + o, n)
+            for i in [*far_first(X), 0]:
+                if o or i:
+                    at = {axis: to, "x": lax.rem(x + i, X)}
+                    remote(s2.at[to], r2.at[slot], s2_send.at[k], s2_recv.at[k], at)
+                    remote(c2.at[to], cr2.at[slot], c2_send.at[k], c2_recv.at[k], at)
+
+        order = [*far_first(n), 0]
+        if k:
+            for o in order:
+                block(o)
+            drained(ra, s1_recv.at[0])
+            for o in order:
+                send(o)
+        else:
+            for o in order:
+                block(o)
+                send(o)
+        r2[slot] = s2[me]
+        cr2[slot] = c2[me]
+
+    fold(1, "y", z, y, Y, sb, rb, cb, rcb, sb2, rb2, cb2, rcb2)
+    fold(0, "z", y, z, Z, sa, ra, ca, rca, sa2, ra2, ca2, rca2)
+
+    def total(k, r2, cr2):
+        drained(r2.at[pl.ds(0, r2.shape[0] - 1)], s2_recv.at[k])
+        drained(cr2.at[pl.ds(0, r2.shape[0] - 1)], c2_recv.at[k])
+        acc, check = r2[0].astype(F32), cr2[0]
+        for i in range(1, r2.shape[0]):
+            acc += r2[i].astype(F32)
+            check += cr2[i]
+        return acc, check
+
+    low, low_check = total(1, rb2, rcb2)
+    top, top_check = total(0, ra2, rca2)
     m = 2 * p + c
-    acc, check = x3[0], xc[0]
-    for i in range(1, X):
-        acc += x3[i]
-        check += xc[i]
-
-    nsend[...] = jnp.sum(acc * acc, axis=0, keepdims=True)
-    grp[m] = acc
-    gc[m] = check
+
+    nsend[...] = jnp.sum(top * top + low * low, axis=0, keepdims=True)
+    grp[m, 0:16, :] = top
+    grp[m, 16:32, :] = low
+    gc[m, 0] = top_check
+    gc[m, 1] = low_check
     order = sorted(
         ((a, b, k) for a in range(Z) for b in range(Y) for k in range(2) if a or b or k),
         key=lambda o: -(min(o[0], Z - o[0]) + min(o[1], Y - o[1])),
@@ -201,11 +206,22 @@
     drained(par, s0_send)
     for ref, sem in (
         (ra, s1_send.at[0]), (rb, s1_send.at[1]), (rca, c1_send.at[0]), (rcb, c1_send.at[1]),
-        (ra2, s2_send.at[0]), (rb2, s2_send.at[1]), (rca2, c2_send.at[0]), (rcb2, c2_send.at[1]),
-        (x3.at[pl.ds(0, X - 1)], x_sem.at[0]), (xc.at[pl.ds(0, X - 1)], x_sem.at[2]),
+        (ra2.at[pl.ds(0, X * Z - 1)], s2_send.at[0]), (rb2.at[pl.ds(0, X * Y - 1)], s2_send.at[1]),
+        (rca2.at[pl.ds(0, X * Z - 1)], c2_send.at[0]), (rcb2.at[pl.ds(0, X * Y - 1)], c2_send.at[1]),
         (grp.at[pl.ds(0, 3)], g_sem.at[0]), (gc.at[pl.ds(0, 3)], g_sem.at[2]), (nrm, n_sem.at[0]),
     ):
         drained(ref, sem)
+
+
+def leave(out_ref, chk_ref, to_ref, chk_to_ref, sem):
+    copies = [
+        pltpu.make_async_copy(out_ref, to_ref, sem.at[0]),
+        pltpu.make_async_copy(chk_ref, chk_to_ref, sem.at[1]),
+    ]
+    for copy in copies:
+        copy.start()
+    for copy in copies:
+        copy.wait()
 
 
 def body(sizes, grads, check_weights):
@@ -227,10 +243,8 @@
             vmem((8, 16), jnp.int32),
             *(vmem((n, 16 * k, LANES), BF) for n, k in ((Y, Z), (Z, Y), (Y - 1, Z), (Z - 1, Y))),
             *(vmem((n, 8, LANES), BF) for n in (Y, Z, Y - 1, Z - 1)),
-            *(vmem((n, 16, LANES), F32) for n in (Z, Y, Z - 1, Y - 1)),
-            *(vmem((n, 1, LANES), F32) for n in (Z, Y, Z - 1, Y - 1)),
-            vmem((X, 32, LANES), F32),
-            vmem((X, 2, 1, LANES), F32),
+            *(vmem((n, 16, LANES), BF) for n in (Z, Y, X * Z, X * Y)),
+            *(vmem((n, 1, LANES), F32) for n in (Z, Y, X * Z, X * Y)),
             vmem((4, 32, LANES), F32),
             vmem((4, 2, 1, LANES), F32),
             vmem((1, LANES), F32),
@@ -244,11 +258,18 @@
             dma((4,)),
             *(dma((2,)) for _ in range(8)),
             dma((4,)),
-            dma((4,)),
             dma((2,)),
         ],
         compiler_params=pltpu.CompilerParams(collective_id=0, has_side_effects=True, vmem_limit_bytes=8 << 20),
     )(pltpu.with_memory_space_constraint(local, HBM), pltpu.with_memory_space_constraint(weights, HBM))
+    out, chk = pl.pallas_call(
+        leave,
+        out_shape=(jax.ShapeDtypeStruct((32, rows), BF), jax.ShapeDtypeStruct((8, 32), BF)),
+        in_specs=[pl.BlockSpec(memory_space=pl.ANY)] * 2,
+        out_specs=(pl.BlockSpec(memory_space=HBM), pl.BlockSpec(memory_space=HBM)),
+        scratch_shapes=[dma((2,))],
+        compiler_params=pltpu.CompilerParams(vmem_limit_bytes=1 << 20),
+    )(out, chk)
     return out.T, chk
 
 

time: 43.4 us -> 41.8 us (0.963)
  local copies, waits for them, and re-layouts: 1.18 us -> 0 us
    unnamed x2 -> x0, local copies, waits for them, and re-layouts: 1.18 us -> none
    pallas_call x1, Pallas kernels: 41.5 us -> 40.4 us  [body(): pl.pallas_call(functools.partial(kernel, sizes, limit), out_shape=(jax.Sh...]
    pallas_call x0 -> x1, Pallas kernels: none -> 0.62 us  [body(): pl.pallas_call(leave, out_shape=(jax.ShapeDtypeStruct((32, rows), BF), ja...]
where the time goes in v3:
time: 41.8 us; the launch traced here: 41.7 us
  Pallas kernels  41.1 us (98%)
  between operations  0.64 us (2%)
    pallas_call x1, Pallas kernels, body(): pl.pallas_call(functools.partial(kernel, sizes, limit), out_shape=(jax.Sh...  40.4 us

profile of v3, /device:TPU:1, one launch (start us, length us, event | category | flops | bytes accessed | tf_op | source)
XLA Modules:
  0.0 41.7 jit_solution(10140374797135043524)
XLA Ops:
  0.6 40.4 %shard_map.41 = (bf16[32,128]{1,0:T(8,128)(2,1)S(1)}, bf16[8,32]{1,0:T(8,128)(2,1)S(1)}) custom-call(bf16[128,4096]{1,0:T(8,128)(2,1)} %bitcast.3, s32[8,16]{1,0:T(8,128)} %bitcast.4), custom_call_target="tpu_custom_call" | custom-call | tf_op jit(solution)/shard_map/pallas_call | solution.py:234
  41.1 0.6 %shard_map.42 = (bf16[32,128]{1,0:T(8,128)(2,1)}, bf16[8,32]{1,0:T(8,128)(2,1)}) custom-call(bf16[32,128]{1,0:T(8,128)(2,1)S(1)} %get-tuple-element.6.out_ref, bf16[8,32]{1,0:T(8,128)(2,1)S(1)} %get-tuple-element.7.chk_ref), custom_call_target="tpu_custom_call" | custom-call | tf_op jit(solution)/shard_map/pallas_call | solution.py:265

commit v4 on v3

--- a/solution.py
+++ b/solution.py
@@ -22,8 +22,8 @@
     return [o for o in far_first(n) if min(o, n - o) <= 2]
 
 
-def kernel(sizes, limit, g_ref, w_ref, out_ref, chk_ref, own, par, wown, wpar, sa, sb, ra, rb, ca, cb, rca, rcb,
-           sa2, sb2, ra2, rb2, ca2, cb2, rca2, rcb2, grp, gc, nsend, nrm, xt, chk, own_sem, w_sem, hop,
+def kernel(sizes, limit, g_ref, w_ref, out_ref, chk_ref, own, away, par, wown, wpar, sa, sb, ra, rb, ca, cb, rca, rcb,
+           sa2, sb2, ra2, rb2, ca2, cb2, rca2, rcb2, grp, gc, nsend, nrm, xt, chk, own_sem, away_sem, w_sem, hop,
            s0_send, s0_recv, s1_send, s1_recv, c1_send, c1_recv, s2_send, s2_recv, c2_send, c2_recv,
            g_sem, n_sem):
     Z, Y, X = sizes
@@ -48,6 +48,9 @@
     weights.start()
     mine = pltpu.make_async_copy(g_ref.at[half], own, own_sem)
     mine.start()
+    rest = pl.ds(pl.multiple_of(other * 64, 64), 64)
+    theirs = pltpu.make_async_copy(g_ref.at[rest], away, away_sem)
+    theirs.start()
 
     barrier = pltpu.get_barrier_semaphore()
     for o in near(Y):
@@ -63,9 +66,9 @@
         signal(hop.at[0], {"y": lax.rem(y + o, Y)})
     for o in near(Z):
         signal(hop.at[1], {"z": lax.rem(z + o, Z)})
-    for q in (0, 2, 3, 1):
-        rows = pl.ds(pl.multiple_of(other * 64 + 16 * q, 16), 16)
-        remote(g_ref.at[rows], par.at[q], s0_send, s0_recv.at[q], {"c": other})
+    theirs.wait()
+    for q in (2, 3, 0, 1):
+        remote(away.at[pl.ds(16 * q, 16)], par.at[q], s0_send, s0_recv.at[q], {"c": other})
     remote(w_ref, wpar, w_sem.at[0], w_sem.at[1], {"c": other})
 
     eye = lax.broadcasted_iota(jnp.int32, (16, 16), 0) == lax.broadcasted_iota(jnp.int32, (16, 16), 1)
@@ -87,7 +90,21 @@
     drained(wpar, w_sem.at[1])
     w_par = columns(wpar)
 
-    for q in (0, 2, 3, 1):
+    def place(t, me, n):
+        return lax.rem(t - me - 2 + 2 * n, n)
+
+    def spread(k, axis, me, n, s, r, h):
+        half_rows = pl.ds(s.shape[1] // 2 * h, s.shape[1] // 2)
+        for o in far_first(n):
+            to = lax.rem(me + o, n)
+            remote(s.at[to, half_rows], r.at[o - 1, half_rows], s1_send.at[k, h], s1_recv.at[k, h], {axis: to})
+
+    def spread_checks(k, axis, me, n, cs, cr):
+        for o in far_first(n):
+            to = lax.rem(me + o, n)
+            remote(cs.at[to], cr.at[o - 1], c1_send.at[k], c1_recv.at[k], {axis: to})
+
+    for q in (2, 3, 0, 1):
         drained(par.at[q], s0_recv.at[q])
         for t in range(Z * YH):
             zt, yt = t // YH, t % YH
@@ -95,42 +112,49 @@
             a = own[16 * q : 16 * q + 16, lanes].astype(F32)
             b = par[q, :, lanes].astype(F32)
             check = jnp.sum(a * w_own[q] + b * w_par[q], axis=0, keepdims=True)
-            to, cto, at, i = (sa, ca, 2 * yt + q, zt) if q < 2 else (sb, cb, zt, 2 * yt + q - 2)
-            to[at, 16 * i : 16 * i + 16, :] = (a + b).astype(BF)
-            cto[at, i : i + 1, :] = check.astype(BF)
+            if q < 2:
+                to, cto, at, tile, i = sa, ca, 2 * yt + q, zt, place(zt, z, Z)
+            else:
+                to, cto, at, tile, i = sb, cb, zt, 2 * yt + q - 2, place(2 * yt + q - 2, y, Y)
+            to[at, pl.ds(pl.multiple_of(16 * i, 16), 16), :] = (a + b).astype(BF)
+            cto[at, tile : tile + 1, :] = check.astype(BF)
         if q == 3:
             pl.semaphore_wait(hop.at[1], len(near(Z)))
-            for o in far_first(Z):
-                to = lax.rem(z + o, Z)
-                remote(sb.at[to], rb.at[o - 1], s1_send.at[1], s1_recv.at[1], {"z": to})
-                remote(cb.at[to], rcb.at[o - 1], c1_send.at[1], c1_recv.at[1], {"z": to})
-        if q == 1:
-            pl.semaphore_wait(hop.at[0], len(near(Y)))
-            for o in far_first(Y):
-                to = lax.rem(y + o, Y)
-                remote(sa.at[to], ra.at[o - 1], s1_send.at[0], s1_recv.at[0], {"y": to})
-                remote(ca.at[to], rca.at[o - 1], c1_send.at[0], c1_recv.at[0], {"y": to})
-
-    def fold(k, axis, held, me, n, s, r, cs, cr, s2, r2, c2, cr2):
+            spread_checks(1, "z", z, Z, cb, rcb)
+            spread(1, "z", z, Z, sb, rb, 0)
+    pl.semaphore_wait(hop.at[0], len(near(Y)))
+    spread_checks(0, "y", y, Y, ca, rca)
+    spread(0, "y", y, Y, sa, ra, 0)
+    spread(1, "z", z, Z, sb, rb, 1)
+    spread(0, "y", y, Y, sa, ra, 1)
+
+    def fold_checks(k, held, cs, cr, c2):
         drained(cr, c1_recv.at[k])
         check = cs[held].astype(F32)
         for o in range(cr.shape[0]):
             check += cr[o].astype(F32)
-        for t in range(n):
+        for t in range(c2.shape[0]):
             c2[t] = check[t : t + 1]
-        if k:
-            drained(r, s1_recv.at[k])
+
+    def arrived(k, r, h):
+        drained(r.at[:, pl.ds(r.shape[1] // 2 * h, r.shape[1] // 2)], s1_recv.at[k, h])
+
+    def offsets(n, h):
+        places = range(n // 2 * h, n // 2 * (h + 1))
+        return sorted(((i + 2) % n for i in places), key=lambda o: -min(o, n - o))
+
+    def block(h, held, me, n, s, r, s2):
+        for o in offsets(n, h):
+            i = (o - 2) % n
+            rows = slice(16 * i, 16 * i + 16)
+            acc = s[held, rows, :].astype(F32)
+            for j in range(r.shape[0]):
+                acc += r[j, rows, :].astype(F32)
+            s2[lax.rem(me + o, n)] = acc.astype(BF)
+
+    def give(k, h, axis, me, n, s2, r2, c2, cr2):
         slot = x * n + me
-
-        def block(o):
-            to = lax.rem(me + o, n)
-            rows = pl.ds(pl.multiple_of(16 * to, 16), 16)
-            acc = s[held, rows, :].astype(F32)
-            for i in range(r.shape[0]):
-                acc += r[i, rows, :].astype(F32)
-            s2[to] = acc.astype(BF)
-
-        def send(o):
+        for o in offsets(n, h):
             to = lax.rem(me + o, n)
             for i in [*far_first(X), 0]:
                 if o or i:
@@ -138,22 +162,22 @@
                     remote(s2.at[to], r2.at[slot], s2_send.at[k], s2_recv.at[k], at)
                     remote(c2.at[to], cr2.at[slot], c2_send.at[k], c2_recv.at[k], at)
 
-        order = [*far_first(n), 0]
-        if k:
-            for o in order:
-                block(o)
-            drained(ra, s1_recv.at[0])
-            for o in order:
-                send(o)
-        else:
-            for o in order:
-                block(o)
-                send(o)
-        r2[slot] = s2[me]
-        cr2[slot] = c2[me]
-
-    fold(1, "y", z, y, Y, sb, rb, cb, rcb, sb2, rb2, cb2, rcb2)
-    fold(0, "z", y, z, Z, sa, ra, ca, rca, sa2, ra2, ca2, rca2)
+    fold_checks(1, z, cb, rcb, cb2)
+    arrived(1, rb, 0)
+    block(0, z, y, Y, sb, rb, sb2)
+    fold_checks(0, y, ca, rca, ca2)
+    arrived(0, ra, 0)
+    give(1, 0, "y", y, Y, sb2, rb2, cb2, rcb2)
+    block(0, y, z, Z, sa, ra, sa2)
+    give(0, 0, "z", z, Z, sa2, ra2, ca2, rca2)
+    arrived(1, rb, 1)
+    block(1, z, y, Y, sb, rb, sb2)
+    give(1, 1, "y", y, Y, sb2, rb2, cb2, rcb2)
+    arrived(0, ra, 1)
+    block(1, y, z, Z, sa, ra, sa2)
+    give(0, 1, "z", z, Z, sa2, ra2, ca2, rca2)
+    rb2[x * Y + y], rcb2[x * Y + y] = sb2[y], cb2[y]
+    ra2[x * Z + z], rca2[x * Z + z] = sa2[z], ca2[z]
 
     def total(k, r2, cr2):
         drained(r2.at[pl.ds(0, r2.shape[0] - 1)], s2_recv.at[k])
@@ -205,7 +229,8 @@
     drained(wown, w_sem.at[0])
     drained(par, s0_send)
     for ref, sem in (
-        (ra, s1_send.at[0]), (rb, s1_send.at[1]), (rca, c1_send.at[0]), (rcb, c1_send.at[1]),
+        *((r.at[:, pl.ds(r.shape[1] // 2 * h, r.shape[1] // 2)], s1_send.at[k, h]) for k, r in ((0, ra), (1, rb)) for h in (0, 1)),
+        (rca, c1_send.at[0]), (rcb, c1_send.at[1]),
         (ra2.at[pl.ds(0, X * Z - 1)], s2_send.at[0]), (rb2.at[pl.ds(0, X * Y - 1)], s2_send.at[1]),
         (rca2.at[pl.ds(0, X * Z - 1)], c2_send.at[0]), (rcb2.at[pl.ds(0, X * Y - 1)], c2_send.at[1]),
         (grp.at[pl.ds(0, 3)], g_sem.at[0]), (gc.at[pl.ds(0, 3)], g_sem.at[2]), (nrm, n_sem.at[0]),
@@ -237,6 +262,7 @@
         in_specs=[pl.BlockSpec(memory_space=HBM)] * 2,
         out_specs=(pl.BlockSpec(memory_space=vmem), pl.BlockSpec(memory_space=vmem)),
         scratch_shapes=[
+            vmem((64, width), BF),
             vmem((64, width), BF),
             vmem((4, 16, width), BF),
             vmem((8, 16), jnp.int32),
@@ -252,11 +278,14 @@
             vmem((LANES, LANES), F32),
             vmem((8, LANES), F32),
             dma,
+            dma,
             dma((3,)),
             pltpu.SemaphoreType.REGULAR((2,)),
             dma,
             dma((4,)),
-            *(dma((2,)) for _ in range(8)),
+            dma((2, 2)),
+            dma((2, 2)),
+            *(dma((2,)) for _ in range(6)),
             dma((4,)),
             dma((2,)),
         ],

time: 41.8 us -> 39.6 us (0.947)
  Pallas kernels: 41.1 us -> 38.8 us
    pallas_call x1, Pallas kernels: 40.4 us -> 38.2 us  [body(): pl.pallas_call(functools.partial(kernel, sizes, limit), out_shape=(jax.Sh...]
where the time goes in v4:
time: 39.6 us; the launch traced here: 39.4 us
  Pallas kernels  38.8 us (98%)
  between operations  0.64 us (2%)
    pallas_call x1, Pallas kernels, body(): pl.pallas_call(functools.partial(kernel, sizes, limit), out_shape=(jax.Sh...  38.2 us

profile of v4, /device:TPU:1, one launch (start us, length us, event | category | flops | bytes accessed | tf_op | source)
XLA Modules:
  0.0 39.4 jit_solution(1746919233809481109)
XLA Ops:
  0.6 38.2 %shard_map.41 = (bf16[32,128]{1,0:T(8,128)(2,1)S(1)}, bf16[8,32]{1,0:T(8,128)(2,1)S(1)}) custom-call(bf16[128,4096]{1,0:T(8,128)(2,1)} %bitcast.3, s32[8,16]{1,0:T(8,128)} %bitcast.4), custom_call_target="tpu_custom_call" | custom-call | tf_op jit(solution)/shard_map/pallas_call | solution.py:259
  38.8 0.6 %shard_map.42 = (bf16[32,128]{1,0:T(8,128)(2,1)}, bf16[8,32]{1,0:T(8,128)(2,1)}) custom-call(bf16[32,128]{1,0:T(8,128)(2,1)S(1)} %get-tuple-element.6.out_ref, bf16[8,32]{1,0:T(8,128)(2,1)S(1)} %get-tuple-element.7.chk_ref), custom_call_target="tpu_custom_call" | custom-call | tf_op jit(solution)/shard_map/pallas_call | solution.py:294

commit v5 on v4

--- a/solution.py
+++ b/solution.py
@@ -11,6 +11,7 @@
 MESH = pl.DeviceIdType.MESH
 BF, F32 = jnp.bfloat16, jnp.float32
 LANES = 128
+GROUPS = 2
 HBM = pltpu.MemorySpace.HBM
 
 
@@ -28,6 +29,7 @@
            g_sem, n_sem):
     Z, Y, X = sizes
     YH = Y // 2
+    groups = min(GROUPS, Z, Y)
     z, y, c, x = (lax.axis_index(a) for a in ("z", "y", "c", "x"))
     yh, p = y // 2, lax.rem(y, 2)
     other = 1 - c
@@ -84,129 +86,156 @@
             cols.append(jnp.broadcast_to(col, (16, LANES)))
         return cols
 
-    weights.wait()
-    w_own = columns(wown)
     mine.wait()
-    drained(wpar, w_sem.at[1])
-    w_par = columns(wpar)
 
     def place(t, me, n):
-        return lax.rem(t - me - 2 + 2 * n, n)
-
-    def spread(k, axis, me, n, s, r, h):
-        half_rows = pl.ds(s.shape[1] // 2 * h, s.shape[1] // 2)
+        d = lax.rem(t - me + n, n)
+        return jnp.where(d >= n // 2, 2 * d - n, n - 1 - 2 * d)
+
+    def offsets(n, g):
+        by_place = sorted(range(n), key=lambda d: rank(d, n))
+        return by_place[n // groups * g : n // groups * (g + 1)]
+
+    def portion(ref, g):
+        size = ref.shape[-2] // groups
+        return pl.ds(size * g, size)
+
+    def spread(k, axis, me, n, s, r, g):
         for o in far_first(n):
             to = lax.rem(me + o, n)
-            remote(s.at[to, half_rows], r.at[o - 1, half_rows], s1_send.at[k, h], s1_recv.at[k, h], {axis: to})
-
-    def spread_checks(k, axis, me, n, cs, cr):
-        for o in far_first(n):
-            to = lax.rem(me + o, n)
-            remote(cs.at[to], cr.at[o - 1], c1_send.at[k], c1_recv.at[k], {axis: to})
-
-    for q in (2, 3, 0, 1):
-        drained(par.at[q], s0_recv.at[q])
+            part = portion(s, g)
+            remote(s.at[to, part], r.at[o - 1, part], s1_send.at[k, g], s1_recv.at[k, g], {axis: to})
+
+    def tiles(q):
         for t in range(Z * YH):
             zt, yt = t // YH, t % YH
             lanes = slice(t * LANES, (t + 1) * LANES)
             a = own[16 * q : 16 * q + 16, lanes].astype(F32)
             b = par[q, :, lanes].astype(F32)
-            check = jnp.sum(a * w_own[q] + b * w_par[q], axis=0, keepdims=True)
+            yield zt, 2 * yt + q % 2, a, b
+
+    y_place = [pl.multiple_of(16 * place(t, y, Y), 16) for t in range(Y)]
+    z_place = [pl.multiple_of(16 * place(t, z, Z), 16) for t in range(Z)]
+    for q in (2, 3, 0, 1):
+        drained(par.at[q], s0_recv.at[q])
+        for zt, yt, a, b in tiles(q):
             if q < 2:
-                to, cto, at, tile, i = sa, ca, 2 * yt + q, zt, place(zt, z, Z)
+                sa[yt, pl.ds(z_place[zt], 16), :] = (a + b).astype(BF)
             else:
-                to, cto, at, tile, i = sb, cb, zt, 2 * yt + q - 2, place(2 * yt + q - 2, y, Y)
-            to[at, pl.ds(pl.multiple_of(16 * i, 16), 16), :] = (a + b).astype(BF)
-            cto[at, tile : tile + 1, :] = check.astype(BF)
+                sb[zt, pl.ds(y_place[yt], 16), :] = (a + b).astype(BF)
         if q == 3:
             pl.semaphore_wait(hop.at[1], len(near(Z)))
-            spread_checks(1, "z", z, Z, cb, rcb)
             spread(1, "z", z, Z, sb, rb, 0)
     pl.semaphore_wait(hop.at[0], len(near(Y)))
-    spread_checks(0, "y", y, Y, ca, rca)
     spread(0, "y", y, Y, sa, ra, 0)
-    spread(1, "z", z, Z, sb, rb, 1)
-    spread(0, "y", y, Y, sa, ra, 1)
-
-    def fold_checks(k, held, cs, cr, c2):
+    for g in range(1, groups):
+        spread(1, "z", z, Z, sb, rb, g)
+        spread(0, "y", y, Y, sa, ra, g)
+
+    weights.wait()
+    w_own = columns(wown)
+    drained(wpar, w_sem.at[1])
+    w_par = columns(wpar)
+    for q in (2, 3, 0, 1):
+        for zt, yt, a, b in tiles(q):
+            check = jnp.sum(a * w_own[q] + b * w_par[q], axis=0, keepdims=True).astype(BF)
+            if q < 2:
+                ca[yt, zt : zt + 1, :] = check
+            else:
+                cb[zt, yt : yt + 1, :] = check
+    for k, axis, me, n, cs, cr in ((1, "z", z, Z, cb, rcb), (0, "y", y, Y, ca, rca)):
+        for o in far_first(n):
+            to = lax.rem(me + o, n)
+            remote(cs.at[to], cr.at[o - 1], c1_send.at[k], c1_recv.at[k], {axis: to})
+
+    def arrived(k, r, g):
+        drained(r.at[:, portion(r, g)], s1_recv.at[k, g])
+
+    def rank(o, n):
+        return 2 * o - n if o >= n // 2 else n - 1 - 2 * o
+
+    def slot_of(o, n):
+        return X * rank(o, n) + x
+
+    def block(g, held, me, n, s, r, s2):
+        for o in offsets(n, g):
+            rows = slice(16 * rank(o, n), 16 * rank(o, n) + 16)
+            acc = s[held, rows, :].astype(F32)
+            for j in range(r.shape[0]):
+                acc += r[j, rows, :].astype(F32)
+            s2[lax.rem(me + o, n)] = acc.astype(BF)
+
+    def give(axis, me, n, os, src, dst, send, recv):
+        for o in os:
+            to = lax.rem(me + o, n)
+            for i in [*far_first(X), 0]:
+                if o or i:
+                    remote(src.at[to], dst.at[slot_of(o, n)], send, recv, {axis: to, "x": lax.rem(x + i, X)})
+
+    def give_tiles(k, g, axis, me, n, s2, r2):
+        give(axis, me, n, offsets(n, g), s2, r2, s2_send.at[k, g], s2_recv.at[k, g])
+
+    for g in range(groups):
+        arrived(1, rb, g)
+        block(g, z, y, Y, sb, rb, sb2)
+        if g == 0:
+            arrived(0, ra, g)
+        give_tiles(1, g, "y", y, Y, sb2, rb2)
+        if g:
+            arrived(0, ra, g)
+        block(g, y, z, Z, sa, ra, sa2)
+        give_tiles(0, g, "z", z, Z, sa2, ra2)
+    rb2[slot_of(0, Y)] = sb2[y]
+    ra2[slot_of(0, Z)] = sa2[z]
+
+    for k, held, axis, me, n, cs, cr, c2, cr2 in (
+        (1, z, "y", y, Y, cb, rcb, cb2, rcb2),
+        (0, y, "z", z, Z, ca, rca, ca2, rca2),
+    ):
         drained(cr, c1_recv.at[k])
         check = cs[held].astype(F32)
         for o in range(cr.shape[0]):
             check += cr[o].astype(F32)
-        for t in range(c2.shape[0]):
+        for t in range(n):
             c2[t] = check[t : t + 1]
-
-    def arrived(k, r, h):
-        drained(r.at[:, pl.ds(r.shape[1] // 2 * h, r.shape[1] // 2)], s1_recv.at[k, h])
-
-    def offsets(n, h):
-        places = range(n // 2 * h, n // 2 * (h + 1))
-        return sorted(((i + 2) % n for i in places), key=lambda o: -min(o, n - o))
-
-    def block(h, held, me, n, s, r, s2):
-        for o in offsets(n, h):
-            i = (o - 2) % n
-            rows = slice(16 * i, 16 * i + 16)
-            acc = s[held, rows, :].astype(F32)
-            for j in range(r.shape[0]):
-                acc += r[j, rows, :].astype(F32)
-            s2[lax.rem(me + o, n)] = acc.astype(BF)
-
-    def give(k, h, axis, me, n, s2, r2, c2, cr2):
-        slot = x * n + me
-        for o in offsets(n, h):
-            to = lax.rem(me + o, n)
-            for i in [*far_first(X), 0]:
-                if o or i:
-                    at = {axis: to, "x": lax.rem(x + i, X)}
-                    remote(s2.at[to], r2.at[slot], s2_send.at[k], s2_recv.at[k], at)
-                    remote(c2.at[to], cr2.at[slot], c2_send.at[k], c2_recv.at[k], at)
-
-    fold_checks(1, z, cb, rcb, cb2)
-    arrived(1, rb, 0)
-    block(0, z, y, Y, sb, rb, sb2)
-    fold_checks(0, y, ca, rca, ca2)
-    arrived(0, ra, 0)
-    give(1, 0, "y", y, Y, sb2, rb2, cb2, rcb2)
-    block(0, y, z, Z, sa, ra, sa2)
-    give(0, 0, "z", z, Z, sa2, ra2, ca2, rca2)
-    arrived(1, rb, 1)
-    block(1, z, y, Y, sb, rb, sb2)
-    give(1, 1, "y", y, Y, sb2, rb2, cb2, rcb2)
-    arrived(0, ra, 1)
-    block(1, y, z, Z, sa, ra, sa2)
-    give(0, 1, "z", z, Z, sa2, ra2, ca2, rca2)
-    rb2[x * Y + y], rcb2[x * Y + y] = sb2[y], cb2[y]
-    ra2[x * Z + z], rca2[x * Z + z] = sa2[z], ca2[z]
-
-    def total(k, r2, cr2):
-        drained(r2.at[pl.ds(0, r2.shape[0] - 1)], s2_recv.at[k])
-        drained(cr2.at[pl.ds(0, r2.shape[0] - 1)], c2_recv.at[k])
-        acc, check = r2[0].astype(F32), cr2[0]
-        for i in range(1, r2.shape[0]):
-            acc += r2[i].astype(F32)
-            check += cr2[i]
-        return acc, check
-
-    low, low_check = total(1, rb2, rcb2)
-    top, top_check = total(0, ra2, rca2)
+        give(axis, me, n, [*far_first(n), 0], c2, cr2, c2_send.at[k], c2_recv.at[k])
+        cr2[slot_of(0, n)] = c2[me]
+
+    def share(r2, g):
+        size = r2.shape[0] // groups
+        return pl.ds(size * g, size - (g == groups - 1))
+
+    low = top = None
+    for g in range(groups):
+        sums = []
+        for k, r2, acc in ((1, rb2, low), (0, ra2, top)):
+            drained(r2.at[share(r2, g)], s2_recv.at[k, g])
+            size = r2.shape[0] // groups
+            for i in range(size * g, size * (g + 1)):
+                acc = r2[i].astype(F32) if acc is None else acc + r2[i].astype(F32)
+            sums.append(acc)
+        low, top = sums
     m = 2 * p + c
 
     nsend[...] = jnp.sum(top * top + low * low, axis=0, keepdims=True)
-    grp[m, 0:16, :] = top
-    grp[m, 16:32, :] = low
-    gc[m, 0] = top_check
-    gc[m, 1] = low_check
     order = sorted(
         ((a, b, k) for a in range(Z) for b in range(Y) for k in range(2) if a or b or k),
         key=lambda o: -(min(o[0], Z - o[0]) + min(o[1], Y - o[1])),
     )
+    far = len(order) // 2
     for j, (dz, dy, dc) in enumerate(order):
         at = {"z": lax.rem(z + dz, Z), "y": lax.rem(y + dy, Y), "c": lax.rem(c + dc, 2)}
-        remote(nsend, nrm.at[j], n_sem.at[0], n_sem.at[1], at)
+        remote(nsend, nrm.at[j], n_sem.at[0], n_sem.at[1 + (j < far)], at)
+    grp[m, 0:16, :] = top
+    grp[m, 16:32, :] = low
     twin = 2 * yh + 1 - p
-    for at in ({"y": twin, "c": other}, {"y": twin, "c": c}, {"y": y, "c": other}):
+    mates = ({"y": twin, "c": other}, {"y": twin, "c": c}, {"y": y, "c": other})
+    for at in mates:
         remote(grp.at[m], grp.at[m], g_sem.at[0], g_sem.at[1], at)
+    for k, cr2 in ((0, rca2), (1, rcb2)):
+        drained(cr2.at[pl.ds(0, cr2.shape[0] - 1)], c2_recv.at[k])
+        gc[m, k] = jnp.sum(cr2[...], axis=0)
+    for at in mates:
         remote(gc.at[m], gc.at[m], g_sem.at[2], g_sem.at[3], at)
     drained(grp.at[pl.ds(0, 3)], g_sem.at[1])
     drained(gc.at[pl.ds(0, 3)], g_sem.at[3])
@@ -219,8 +248,10 @@
     turned = pltpu.roll(chk[...], lax.rem(LANES - 32 * m, LANES), 1)[:, 0:32]
     columns_out = xt[pl.ds(pl.multiple_of(32 * m, 32), 32), :]
 
-    drained(nrm, n_sem.at[1])
-    square = nsend[...] + jnp.sum(nrm[...], axis=0)
+    drained(nrm.at[pl.ds(far, len(order) - far)], n_sem.at[1])
+    square = nsend[...] + jnp.sum(nrm[far:], axis=0)
+    drained(nrm.at[pl.ds(0, far)], n_sem.at[2])
+    square += jnp.sum(nrm[:far], axis=0)
     square = jnp.sum(square, axis=1, keepdims=True)
     factor = jnp.minimum(1.0, limit / jnp.sqrt(square + 1e-06))
     out_ref[...] = (columns_out * factor).astype(BF)
@@ -229,9 +260,9 @@
     drained(wown, w_sem.at[0])
     drained(par, s0_send)
     for ref, sem in (
-        *((r.at[:, pl.ds(r.shape[1] // 2 * h, r.shape[1] // 2)], s1_send.at[k, h]) for k, r in ((0, ra), (1, rb)) for h in (0, 1)),
+        *((r.at[:, portion(r, g)], s1_send.at[k, g]) for k, r in ((0, ra), (1, rb)) for g in range(groups)),
+        *((r.at[share(r, g)], s2_send.at[k, g]) for k, r in ((0, ra2), (1, rb2)) for g in range(groups)),
         (rca, c1_send.at[0]), (rcb, c1_send.at[1]),
-        (ra2.at[pl.ds(0, X * Z - 1)], s2_send.at[0]), (rb2.at[pl.ds(0, X * Y - 1)], s2_send.at[1]),
         (rca2.at[pl.ds(0, X * Z - 1)], c2_send.at[0]), (rcb2.at[pl.ds(0, X * Y - 1)], c2_send.at[1]),
         (grp.at[pl.ds(0, 3)], g_sem.at[0]), (gc.at[pl.ds(0, 3)], g_sem.at[2]), (nrm, n_sem.at[0]),
     ):
@@ -283,11 +314,16 @@
             pltpu.SemaphoreType.REGULAR((2,)),
             dma,
             dma((4,)),
-            dma((2, 2)),
-            dma((2, 2)),
-            *(dma((2,)) for _ in range(6)),
+            dma((2, GROUPS)),
+            dma((2, GROUPS)),
+            dma((2,)),
+            dma((2,)),
+            dma((2, GROUPS)),
+            dma((2, GROUPS)),
+            dma((2,)),
+            dma((2,)),
             dma((4,)),
-            dma((2,)),
+            dma((3,)),
         ],
         compiler_params=pltpu.CompilerParams(collective_id=0, has_side_effects=True, vmem_limit_bytes=8 << 20),
     )(pltpu.with_memory_space_constraint(local, HBM), pltpu.with_memory_space_constraint(weights, HBM))

time: 39.6 us -> 38.4 us (0.970)
  Pallas kernels: 38.8 us -> 37.6 us
    pallas_call x1, Pallas kernels: 38.2 us -> 37 us  [body(): pl.pallas_call(functools.partial(kernel, sizes, limit), out_shape=(jax.Sh...]
where the time goes in v5:
time: 38.4 us; the launch traced here: 38.3 us
  Pallas kernels  37.6 us (98%)
  between operations  0.64 us (2%)
    pallas_call x1, Pallas kernels, body(): pl.pallas_call(functools.partial(kernel, sizes, limit), out_shape=(jax.Sh...  37 us

profile of v5, /device:TPU:1, one launch (start us, length us, event | category | flops | bytes accessed | tf_op | source)
XLA Modules:
  0.0 38.3 jit_solution(14388899619495299011)
XLA Ops:
  0.6 37.0 %shard_map.41 = (bf16[32,128]{1,0:T(8,128)(2,1)S(1)}, bf16[8,32]{1,0:T(8,128)(2,1)S(1)}) custom-call(bf16[128,4096]{1,0:T(8,128)(2,1)} %bitcast.3, s32[8,16]{1,0:T(8,128)} %bitcast.4), custom_call_target="tpu_custom_call" | custom-call | tf_op jit(solution)/shard_map/pallas_call | solution.py:290
  37.7 0.6 %shard_map.42 = (bf16[32,128]{1,0:T(8,128)(2,1)}, bf16[8,32]{1,0:T(8,128)(2,1)}) custom-call(bf16[32,128]{1,0:T(8,128)(2,1)S(1)} %get-tuple-element.6.out_ref, bf16[8,32]{1,0:T(8,128)(2,1)S(1)} %get-tuple-element.7.chk_ref), custom_call_target="tpu_custom_call" | custom-call | tf_op jit(solution)/shard_map/pallas_call | solution.py:330

commit v6 on v5

--- a/solution.py
+++ b/solution.py
@@ -118,11 +118,14 @@
     z_place = [pl.multiple_of(16 * place(t, z, Z), 16) for t in range(Z)]
     for q in (2, 3, 0, 1):
         drained(par.at[q], s0_recv.at[q])
-        for zt, yt, a, b in tiles(q):
+        for t in range(Z * YH):
+            zt, yt = t // YH, 2 * (t % YH) + q % 2
+            lanes = slice(t * LANES, (t + 1) * LANES)
+            both = own[16 * q : 16 * q + 16, lanes] + par[q, :, lanes]
             if q < 2:
-                sa[yt, pl.ds(z_place[zt], 16), :] = (a + b).astype(BF)
+                sa[yt, pl.ds(z_place[zt], 16), :] = both
             else:
-                sb[zt, pl.ds(y_place[yt], 16), :] = (a + b).astype(BF)
+                sb[zt, pl.ds(y_place[yt], 16), :] = both
         if q == 3:
             pl.semaphore_wait(hop.at[1], len(near(Z)))
             spread(1, "z", z, Z, sb, rb, 0)

time: 38.4 us -> 38.4 us (level)
  no operation moved by 1% of the time
where the time goes in v6:
time: 38.4 us; the launch traced here: 38.3 us
  Pallas kernels  37.6 us (98%)
  between operations  0.64 us (2%)
    pallas_call x1, Pallas kernels, body(): pl.pallas_call(functools.partial(kernel, sizes, limit), out_shape=(jax.Sh...  37 us

profile of v6, /device:TPU:1, one launch (start us, length us, event | category | flops | bytes accessed | tf_op | source)
XLA Modules:
  0.0 38.3 jit_solution(3603604797301083987)
XLA Ops:
  0.6 37.0 %shard_map.41 = (bf16[32,128]{1,0:T(8,128)(2,1)S(1)}, bf16[8,32]{1,0:T(8,128)(2,1)S(1)}) custom-call(bf16[128,4096]{1,0:T(8,128)(2,1)} %bitcast.3, s32[8,16]{1,0:T(8,128)} %bitcast.4), custom_call_target="tpu_custom_call" | custom-call | tf_op jit(solution)/shard_map/pallas_call | solution.py:293
  37.7 0.6 %shard_map.42 = (bf16[32,128]{1,0:T(8,128)(2,1)}, bf16[8,32]{1,0:T(8,128)(2,1)}) custom-call(bf16[32,128]{1,0:T(8,128)(2,1)S(1)} %get-tuple-element.6.out_ref, bf16[8,32]{1,0:T(8,128)(2,1)S(1)} %get-tuple-element.7.chk_ref), custom_call_target="tpu_custom_call" | custom-call | tf_op jit(solution)/shard_map/pallas_call | solution.py:333

commit v7 on v6

--- a/solution.py
+++ b/solution.py
@@ -45,14 +45,14 @@
     def drained(ref, sem):
         pltpu.make_async_copy(ref, ref, sem).wait()
 
-    half = pl.ds(pl.multiple_of(c * 64, 64), 64)
-    weights = pltpu.make_async_copy(w_ref, wown, w_sem.at[2])
-    weights.start()
-    mine = pltpu.make_async_copy(g_ref.at[half], own, own_sem)
-    mine.start()
     rest = pl.ds(pl.multiple_of(other * 64, 64), 64)
     theirs = pltpu.make_async_copy(g_ref.at[rest], away, away_sem)
     theirs.start()
+    half = pl.ds(pl.multiple_of(c * 64, 64), 64)
+    mine = pltpu.make_async_copy(g_ref.at[half], own, own_sem)
+    mine.start()
+    weights = pltpu.make_async_copy(w_ref, wown, w_sem.at[2])
+    weights.start()
 
     barrier = pltpu.get_barrier_semaphore()
     for o in near(Y):
@@ -225,7 +225,7 @@
         ((a, b, k) for a in range(Z) for b in range(Y) for k in range(2) if a or b or k),
         key=lambda o: -(min(o[0], Z - o[0]) + min(o[1], Y - o[1])),
     )
-    far = len(order) // 2
+    far = len(order) // 8
     for j, (dz, dy, dc) in enumerate(order):
         at = {"z": lax.rem(z + dz, Z), "y": lax.rem(y + dy, Y), "c": lax.rem(c + dc, 2)}
         remote(nsend, nrm.at[j], n_sem.at[0], n_sem.at[1 + (j < far)], at)

time: 38.4 us -> 38.4 us (level)
  no operation moved by 1% of the time
where the time goes in v7:
time: 38.4 us; the launch traced here: 38.2 us
  Pallas kernels  37.6 us (98%)
  between operations  0.64 us (2%)
    pallas_call x1, Pallas kernels, body(): pl.pallas_call(functools.partial(kernel, sizes, limit), out_shape=(jax.Sh...  37 us

profile of v7, /device:TPU:1, one launch (start us, length us, event | category | flops | bytes accessed | tf_op | source)
XLA Modules:
  0.0 38.2 jit_solution(9884999083537246440)
XLA Ops:
  0.6 37.0 %shard_map.41 = (bf16[32,128]{1,0:T(8,128)(2,1)S(1)}, bf16[8,32]{1,0:T(8,128)(2,1)S(1)}) custom-call(bf16[128,4096]{1,0:T(8,128)(2,1)} %bitcast.3, s32[8,16]{1,0:T(8,128)} %bitcast.4), custom_call_target="tpu_custom_call" | custom-call | tf_op jit(solution)/shard_map/pallas_call | solution.py:293
  37.6 0.6 %shard_map.42 = (bf16[32,128]{1,0:T(8,128)(2,1)}, bf16[8,32]{1,0:T(8,128)(2,1)}) custom-call(bf16[32,128]{1,0:T(8,128)(2,1)S(1)} %get-tuple-element.6.out_ref, bf16[8,32]{1,0:T(8,128)(2,1)S(1)} %get-tuple-element.7.chk_ref), custom_call_target="tpu_custom_call" | custom-call | tf_op jit(solution)/shard_map/pallas_call | solution.py:333
